TPU v7x, 128 devices: a whole 4x4x4 slice. The times are simulated.
128 devices in a mesh: row: 8 (over y, z_hi), col: 16 (over z_lo, x, core).
Axes of the slice: x: 4, y: 4, z: 4 (z_hi: 2, z_lo: 2; z = z_hi * 2 + z_lo), core: 2. Of those that a mesh axis runs over, the one named last changes fastest.
Arguments:
- points: float32 [32, 49152], P(None, ('row', 'col')), may hold values from -6 to 6
- lengthscale: float32 [32], replicated, may hold values from 1.5 to 6
- outputscale: float32 [1], replicated, may hold values from 0.1 to 0.6
- noise: float32 [1], replicated, may hold values from 0.2 to 2
- rhs: float32 [17, 49152], P(None, ('row', 'col')), may hold values from -6 to 6
- iterate: float32 [17, 49152], P(None, ('row', 'col')), may hold values from -3 to 3
- residual: float32 [17, 49152], P(None, ('row', 'col')), may hold values from -27 to 27
- direction: float32 [17, 49152], P(None, ('row', 'col')), may hold values from -27 to 27
Outputs:
- iterate_next: float32 [17, 49152], P(None, ('row', 'col'))
- residual_next: float32 [17, 49152], P(None, ('row', 'col'))
- direction_next: float32 [17, 49152], P(None, ('row', 'col'))
- length_terms: float32 [32, 49152], P(None, ('row', 'col'))
All inputs are finite; a program needn't handle non-finite values.
Results may differ from a plain program's by a relative error of at most 0.0003.
Values sent between devices are 32-bit elements; how exact they have to be, the bound alone decides.
A program may use at most 64 MiB of HBM per device.

v0:
```python
import math

import jax
import jax.numpy as jnp
from jax import lax
from jax.sharding import PartitionSpec as P


def tile_update(totals, column_block, row_scaled, row_sqnorm, row_iterate, amplitude):
    product, first_moment, second_moment, row_total = totals
    col_scaled, col_direction, col_coeff = column_block
    col_sqnorm = jnp.sum(col_scaled * col_scaled, axis=0)
    inner_prod = jnp.einsum("dr,dc->rc", row_scaled, col_scaled, precision=lax.Precision.HIGHEST)
    kernel = amplitude * jnp.exp(
        -0.5 * (row_sqnorm[:, None] + col_sqnorm[None, :] - 2.0 * inner_prod)
    )
    product = product + jnp.einsum(
        "sc,rc->sr", col_direction, kernel, precision=lax.Precision.HIGHEST
    )
    weight = jnp.einsum("sr,sc->rc", row_iterate, col_coeff, precision=lax.Precision.HIGHEST)
    energy = kernel * weight
    stacked = jnp.concatenate([col_scaled, col_scaled * col_scaled], axis=0)
    moments = jnp.einsum("dc,rc->dr", stacked, energy, precision=lax.Precision.HIGHEST)
    dim_count = col_scaled.shape[0]
    first_moment = first_moment + moments[:dim_count]
    second_moment = second_moment + moments[dim_count:]
    row_total = row_total + jnp.sum(energy, axis=1)
    return (product, first_moment, second_moment, row_total)


def row_pass(row_scaled, row_iterate, amplitude):
    row_sqnorm = jnp.sum(row_scaled * row_scaled, axis=0)

    def fold_columns(totals, pieces, first_index):
        col_scaled, col_direction, col_coeff = pieces
        piece_width = col_scaled.shape[1]
        block_width = math.gcd(piece_width, 512)
        block_count = piece_width // block_width

        def split_cols(values):
            return jnp.moveaxis(values.reshape(values.shape[0], block_count, block_width), 1, 0)

        def scan_step(carried, column_block):
            return (
                tile_update(carried, column_block, row_scaled, row_sqnorm, row_iterate, amplitude),
                None,
            )

        totals, unused = lax.scan(
            scan_step,
            totals,
            (split_cols(col_scaled), split_cols(col_direction), split_cols(col_coeff)),
        )
        return totals

    rows_here = row_scaled.shape[1]
    initial = (
        jnp.zeros((row_iterate.shape[0], rows_here), jnp.float32),
        jnp.zeros((row_scaled.shape[0], rows_here), jnp.float32),
        jnp.zeros((row_scaled.shape[0], rows_here), jnp.float32),
        jnp.zeros((rows_here,), jnp.float32),
    )
    return (fold_columns, initial)


def combine_rows(totals, row_scaled):
    product, first_moment, second_moment, row_total = totals
    gradient = (
        row_scaled * row_scaled * row_total[None, :]
        - 2.0 * row_scaled * first_moment
        + second_moment
    )
    return (product, gradient)


def on_device(points, lengthscale, outputscale, noise, rhs, iterate, residual, direction):
    probes = rhs.shape[0] - 1
    scaled = points / lengthscale[:, None]
    coefficient = jnp.concatenate([iterate[:1], -rhs[1:] / probes], axis=0)
    amplitude = outputscale[0]
    norm_now = lax.psum(jnp.sum(residual * residual, axis=1), ("row", "col"))
    row_scaled, row_iterate = (
        lax.all_gather(scaled, "col", axis=1, tiled=True),
        lax.all_gather(iterate, "col", axis=1, tiled=True),
    )
    fold_columns, initial = row_pass(row_scaled, row_iterate, amplitude)
    totals = fold_columns(
        initial,
        (
            lax.all_gather(scaled, "row", axis=1, tiled=True),
            lax.all_gather(direction, "row", axis=1, tiled=True),
            lax.all_gather(coefficient, "row", axis=1, tiled=True),
        ),
        jnp.int32(0),
    )
    row_partial = combine_rows(totals, row_scaled)
    kernel_part, grad_sum = (
        lax.psum_scatter(row_partial[0], "col", scatter_dimension=1, tiled=True),
        lax.psum_scatter(row_partial[1], "col", scatter_dimension=1, tiled=True),
    )
    kernel_image = kernel_part + noise[0] * direction
    curvature = lax.psum(jnp.sum(direction * kernel_image, axis=1), ("row", "col"))
    step_size = norm_now / curvature
    residual_next = residual - step_size[:, None] * kernel_image
    norm_next = lax.psum(jnp.sum(residual_next * residual_next, axis=1), ("row", "col"))
    iterate_next = iterate + step_size[:, None] * direction
    direction_next = residual_next + (norm_next / (norm_now + 1e-06))[:, None] * direction
    length_terms = 0.5 * grad_sum / lengthscale[:, None]
    return (iterate_next, residual_next, direction_next, length_terms)


def solution(mesh):
    placed = (
        P(None, ("row", "col")),
        P(),
        P(),
        P(),
        P(None, ("row", "col")),
        P(None, ("row", "col")),
        P(None, ("row", "col")),
        P(None, ("row", "col")),
    )
    return jax.shard_map(
        on_device,
        mesh=mesh,
        in_specs=placed,
        out_specs=(
            P(None, ("row", "col")),
            P(None, ("row", "col")),
            P(None, ("row", "col")),
            P(None, ("row", "col")),
        ),
        check_vma=False,
    )
```

profile of v0, /device:TPU:1, one launch (start us, length us, event | category | flops | bytes accessed | tf_op | source)
XLA Modules:
  0.0 645.0 jit_solution(6010158340877558717)
XLA Ops:
  8.1 24.9 %all_gather.16 = f32[32,6144]{1,0:T(8,128)} all-gather(f32[32,384]{1,0:T(8,128)S(1)} %broadcast_divide_fusion), channel_id=1, replica_groups=mesh['row'=8,'col'=16] {'col'}, dimensions={1}, use_global_device_ids=true | all-gather | bytes 835584 | tf_op jit(solution)/shard_map/all_gather | solution.py:83
  33.0 29.2 %all_gather.17 = f32[32,3072]{1,0:T(8,128)S(1)} all-gather(f32[32,384]{1,0:T(8,128)S(1)} %broadcast_divide_fusion), channel_id=1, replica_groups=mesh['row'=8,'col'=16] {'row'}, dimensions={1}, use_global_device_ids=true | all-gather | bytes 442368 | tf_op jit(solution)/shard_map/all_gather | solution.py:90
  63.0 23.8 %all_gather.19 = f32[17,6144]{1,0:T(8,128)S(1)} all-gather(f32[17,384]{1,0:T(8,128)} %param.15), channel_id=1, replica_groups=mesh['row'=8,'col'=16] {'col'}, dimensions={1}, use_global_device_ids=true | all-gather | bytes 443904 | tf_op jit(solution)/shard_map/all_gather | solution.py:84
  86.8 28.8 %all_gather.15 = f32[17,3072]{1,0:T(8,128)S(1)} all-gather(f32[17,384]{1,0:T(8,128)} %param.17), channel_id=1, replica_groups=mesh['row'=8,'col'=16] {'row'}, dimensions={1}, use_global_device_ids=true | all-gather | bytes 235008 | tf_op jit(solution)/shard_map/all_gather | solution.py:91
  119.4 28.2 %all_gather.18 = f32[17,3072]{1,0:T(8,128)S(1)} all-gather(f32[17,384]{1,0:T(8,128)S(1)} %pad_maximum_fusion), channel_id=1, replica_groups=mesh['row'=8,'col'=16] {'row'}, dimensions={1}, use_global_device_ids=true | all-gather | bytes 235008 | tf_op jit(solution)/shard_map/all_gather | solution.py:92
  147.8 283.7 %while.17 = (s32[]{:T(128)}, f32[17,6144]{1,0:T(8,128)S(1)}, f32[32,6144]{1,0:T(8,128)S(1)}, f32[32,6144]{1,0:T(8,128)S(1)}, f32[6144]{0:T(1024)S(1)}, /*index=5...) while((s32[]{:T(128)}, f32[17,6144]{1,0:T(8,128)S(1)}, ...), condition=%wide.region_6.7_spmd.clone, body=%wide.region_3.6_spmd.clone.sunk | while | flops 4930422272 | bytes 122503360 | solution.py:49
  149.0 16.4 %fusion.29 = f32[6144,512]{0,1:T(8,128)} fusion(f32[32,6144]{1,0:T(8,128)} %get-tuple-element.287, f32[512]{0:T(512)S(1)} %get-tuple-element.242, f32[6144]{0:T(1024)S(1)} %get-tuple-element.285, f32[]{:T(128)} %get-tuple-element.284, f32[1,32,512]{2,0,1:T(1,128)S(1)} %constant_dynamic-slice_fusion.5), kind=kOutput, calls=%fused_computation.4.clone.1 | convolution fusion | flops 1223688192 | bytes 13461508 | tf_op jit(solution)/shard_map/while/body/eval_jaxpr/dr,dc->rc/dot_general | solution.py:13
  166.6 9.2 %convolution_add_fusion.2 = f32[17,6144]{1,0:T(8,128)S(1)} fusion(f32[6144,512]{0,1:T(8,128)} %fusion.29, f32[17,6144]{1,0:T(8,128)S(1)} %get-tuple-element.265, pred[]{:T(512)S(6)} %compare.3, f32[1,17,512]{2,0,1:T(1,128)S(1)} %get-tuple-element.243), kind=kOutput, calls=%fused_computation.5.clone.1 | convolution fusion | flops 641937408 | bytes 13453313 | tf_op jit(solution)/shard_map/while/body/eval_jaxpr/sc,rc->sr/dot_general | solution.py:17
  175.8 11.1 %fusion.30 = (f32[6144]{0:T(1024)S(1)}, f32[6144,512]{0,1:T(8,128)S(1)}) fusion(f32[6144,512]{0,1:T(8,128)S(1)} %copy-done, f32[17,6144]{1,0:T(8,128)S(1)} %get-tuple-element.289, f32[1,17,512]{2,0,1:T(1,128)S(1)} %get-tuple-element.244), kind=kOutput, calls=%fused_computation.36.clone.1 | convolution fusion | flops 648013824 | bytes 25643008 | tf_op jit(solution)/shard_map/while/body/eval_jaxpr/sr,sc->rc/dot_general | solution.py:20
  196.2 16.4 %fusion.29 = f32[6144,512]{0,1:T(8,128)} fusion(f32[32,6144]{1,0:T(8,128)} %get-tuple-element.287, f32[512]{0:T(512)S(1)} %get-tuple-element.242, f32[6144]{0:T(1024)S(1)} %get-tuple-element.285, f32[]{:T(128)} %get-tuple-element.284, f32[1,32,512]{2,0,1:T(1,128)S(1)} %constant_dynamic-slice_fusion.5), kind=kOutput, calls=%fused_computation.4.clone.1 | convolution fusion | flops 1223688192 | bytes 13461508 | tf_op jit(solution)/shard_map/while/body/eval_jaxpr/dr,dc->rc/dot_general | solution.py:13
  213.8 9.2 %convolution_add_fusion.2 = f32[17,6144]{1,0:T(8,128)S(1)} fusion(f32[6144,512]{0,1:T(8,128)} %fusion.29, f32[17,6144]{1,0:T(8,128)S(1)} %get-tuple-element.265, pred[]{:T(512)S(6)} %compare.3, f32[1,17,512]{2,0,1:T(1,128)S(1)} %get-tuple-element.243), kind=kOutput, calls=%fused_computation.5.clone.1 | convolution fusion | flops 641937408 | bytes 13453313 | tf_op jit(solution)/shard_map/while/body/eval_jaxpr/sc,rc->sr/dot_general | solution.py:17
  223.0 11.1 %fusion.30 = (f32[6144]{0:T(1024)S(1)}, f32[6144,512]{0,1:T(8,128)S(1)}) fusion(f32[6144,512]{0,1:T(8,128)S(1)} %copy-done, f32[17,6144]{1,0:T(8,128)S(1)} %get-tuple-element.289, f32[1,17,512]{2,0,1:T(1,128)S(1)} %get-tuple-element.244), kind=kOutput, calls=%fused_computation.36.clone.1 | convolution fusion | flops 648013824 | bytes 25643008 | tf_op jit(solution)/shard_map/while/body/eval_jaxpr/sr,sc->rc/dot_general | solution.py:20
  243.5 16.4 %fusion.29 = f32[6144,512]{0,1:T(8,128)} fusion(f32[32,6144]{1,0:T(8,128)} %get-tuple-element.287, f32[512]{0:T(512)S(1)} %get-tuple-element.242, f32[6144]{0:T(1024)S(1)} %get-tuple-element.285, f32[]{:T(128)} %get-tuple-element.284, f32[1,32,512]{2,0,1:T(1,128)S(1)} %constant_dynamic-slice_fusion.5), kind=kOutput, calls=%fused_computation.4.clone.1 | convolution fusion | flops 1223688192 | bytes 13461508 | tf_op jit(solution)/shard_map/while/body/eval_jaxpr/dr,dc->rc/dot_general | solution.py:13
  261.1 9.2 %convolution_add_fusion.2 = f32[17,6144]{1,0:T(8,128)S(1)} fusion(f32[6144,512]{0,1:T(8,128)} %fusion.29, f32[17,6144]{1,0:T(8,128)S(1)} %get-tuple-element.265, pred[]{:T(512)S(6)} %compare.3, f32[1,17,512]{2,0,1:T(1,128)S(1)} %get-tuple-element.243), kind=kOutput, calls=%fused_computation.5.clone.1 | convolution fusion | flops 641937408 | bytes 13453313 | tf_op jit(solution)/shard_map/while/body/eval_jaxpr/sc,rc->sr/dot_general | solution.py:17
  270.3 11.1 %fusion.30 = (f32[6144]{0:T(1024)S(1)}, f32[6144,512]{0,1:T(8,128)S(1)}) fusion(f32[6144,512]{0,1:T(8,128)S(1)} %copy-done, f32[17,6144]{1,0:T(8,128)S(1)} %get-tuple-element.289, f32[1,17,512]{2,0,1:T(1,128)S(1)} %get-tuple-element.244), kind=kOutput, calls=%fused_computation.36.clone.1 | convolution fusion | flops 648013824 | bytes 25643008 | tf_op jit(solution)/shard_map/while/body/eval_jaxpr/sr,sc->rc/dot_general | solution.py:20
  290.8 16.4 %fusion.29 = f32[6144,512]{0,1:T(8,128)} fusion(f32[32,6144]{1,0:T(8,128)} %get-tuple-element.287, f32[512]{0:T(512)S(1)} %get-tuple-element.242, f32[6144]{0:T(1024)S(1)} %get-tuple-element.285, f32[]{:T(128)} %get-tuple-element.284, f32[1,32,512]{2,0,1:T(1,128)S(1)} %constant_dynamic-slice_fusion.5), kind=kOutput, calls=%fused_computation.4.clone.1 | convolution fusion | flops 1223688192 | bytes 13461508 | tf_op jit(solution)/shard_map/while/body/eval_jaxpr/dr,dc->rc/dot_general | solution.py:13
  317.6 11.1 %fusion.30 = (f32[6144]{0:T(1024)S(1)}, f32[6144,512]{0,1:T(8,128)S(1)}) fusion(f32[6144,512]{0,1:T(8,128)S(1)} %copy-done, f32[17,6144]{1,0:T(8,128)S(1)} %get-tuple-element.289, f32[1,17,512]{2,0,1:T(1,128)S(1)} %get-tuple-element.244), kind=kOutput, calls=%fused_computation.36.clone.1 | convolution fusion | flops 648013824 | bytes 25643008 | tf_op jit(solution)/shard_map/while/body/eval_jaxpr/sr,sc->rc/dot_general | solution.py:20
  338.0 16.4 %fusion.29 = f32[6144,512]{0,1:T(8,128)} fusion(f32[32,6144]{1,0:T(8,128)} %get-tuple-element.287, f32[512]{0:T(512)S(1)} %get-tuple-element.242, f32[6144]{0:T(1024)S(1)} %get-tuple-element.285, f32[]{:T(128)} %get-tuple-element.284, f32[1,32,512]{2,0,1:T(1,128)S(1)} %constant_dynamic-slice_fusion.5), kind=kOutput, calls=%fused_computation.4.clone.1 | convolution fusion | flops 1223688192 | bytes 13461508 | tf_op jit(solution)/shard_map/while/body/eval_jaxpr/dr,dc->rc/dot_general | solution.py:13
  364.8 11.1 %fusion.30 = (f32[6144]{0:T(1024)S(1)}, f32[6144,512]{0,1:T(8,128)S(1)}) fusion(f32[6144,512]{0,1:T(8,128)S(1)} %copy-done, f32[17,6144]{1,0:T(8,128)S(1)} %get-tuple-element.289, f32[1,17,512]{2,0,1:T(1,128)S(1)} %get-tuple-element.244), kind=kOutput, calls=%fused_computation.36.clone.1 | convolution fusion | flops 648013824 | bytes 25643008 | tf_op jit(solution)/shard_map/while/body/eval_jaxpr/sr,sc->rc/dot_general | solution.py:20
  385.3 16.4 %fusion.29 = f32[6144,512]{0,1:T(8,128)} fusion(f32[32,6144]{1,0:T(8,128)} %get-tuple-element.287, f32[512]{0:T(512)S(1)} %get-tuple-element.242, f32[6144]{0:T(1024)S(1)} %get-tuple-element.285, f32[]{:T(128)} %get-tuple-element.284, f32[1,32,512]{2,0,1:T(1,128)S(1)} %constant_dynamic-slice_fusion.5), kind=kOutput, calls=%fused_computation.4.clone.1 | convolution fusion | flops 1223688192 | bytes 13461508 | tf_op jit(solution)/shard_map/while/body/eval_jaxpr/dr,dc->rc/dot_general | solution.py:13
  412.1 11.1 %fusion.30 = (f32[6144]{0:T(1024)S(1)}, f32[6144,512]{0,1:T(8,128)S(1)}) fusion(f32[6144,512]{0,1:T(8,128)S(1)} %copy-done, f32[17,6144]{1,0:T(8,128)S(1)} %get-tuple-element.289, f32[1,17,512]{2,0,1:T(1,128)S(1)} %get-tuple-element.244), kind=kOutput, calls=%fused_computation.36.clone.1 | convolution fusion | flops 648013824 | bytes 25643008 | tf_op jit(solution)/shard_map/while/body/eval_jaxpr/sr,sc->rc/dot_general | solution.py:20
  435.5 66.9 %reduce-scatter.3.cloned.1.call-done = f32[17,384]{1,0:T(8,128)} async-done(((f32[17,6144]{1,0:T(8,128)}), f32[17,384]{1,0:T(8,128)}) %reduce-scatter.3.cloned.1.call-update) | async-done | bytes 26128 | tf_op jit(solution)/shard_map/reduce_scatter | solution.py:98
  503.2 68.7 %all-reduce = (f32[17]{0:T(128)S(1)}, f32[17]{0:T(128)S(1)}) all-reduce(f32[17]{0:T(128)S(1)} %multiply_reduce_fusion.4, f32[17]{0:T(128)S(1)} %multiply_reduce_fusion.3), channel_id=1, replica_groups=mesh['row'=8,'col'=16] {'row','col'}, use_global_device_ids=true, to_apply=%region_1.0 | all-reduce | flops 34 | bytes 272 | tf_op jit(solution)/shard_map/psum | solution.py:81
  573.6 62.4 %psum.23 = f32[17]{0:T(128)S(1)} all-reduce(f32[17]{0:T(128)S(1)} %get-tuple-element.150), channel_id=1, replica_groups=mesh['row'=8,'col'=16] {'row','col'}, use_global_device_ids=true, to_apply=%region_11.12 | all-reduce | flops 17 | bytes 136 | tf_op jit(solution)/shard_map/psum | solution.py:105
  (94 shorter events, 104.2 us)
Async XLA Ops:
  7.2 495.2 %reduce-scatter.3.cloned.1.call-start = ((), (), s32[]{:S(2)}) async-start(), calls=%async_computation.2 | async-start | bytes 626688 | tf_op jit(solution)/shard_map/reduce_scatter | solution.py:98
  147.8 287.6 %copy-start.5 = (f32[17,384]{1,0:T(8,128)S(1)}, f32[17,384]{1,0:T(8,128)}, u32[]{:S(2)}) copy-start(f32[17,384]{1,0:T(8,128)} %param.16) | copy-start | bytes 78340
  147.8 354.6 %copy-start.2 = (f32[17,384]{1,0:T(8,128)S(1)}, f32[17,384]{1,0:T(8,128)}, u32[]{:S(2)}) copy-start(f32[17,384]{1,0:T(8,128)} %param.17) | copy-start | bytes 78340
  147.8 424.2 %copy-start.3 = (f32[17,384]{1,0:T(8,128)S(1)}, f32[17,384]{1,0:T(8,128)}, u32[]{:S(2)}) copy-start(f32[17,384]{1,0:T(8,128)} %param.15) | copy-start | bytes 78340
  147.8 488.9 %copy-start.6 = (f32[32]{0:T(128)S(1)}, f32[32]{0:T(128)}, u32[]{:S(2)}) copy-start(f32[32]{0:T(128)} %param.11) | copy-start | bytes 388
  165.4 10.4 %copy-start = (f32[6144,512]{0,1:T(8,128)S(1)}, f32[6144,512]{0,1:T(8,128)}, u32[]{:S(2)}) copy-start(f32[6144,512]{0,1:T(8,128)} %fusion.29) | copy-start | bytes 37748740 | tf_op jit(solution)/shard_map/while
  212.6 10.4 %copy-start = (f32[6144,512]{0,1:T(8,128)S(1)}, f32[6144,512]{0,1:T(8,128)}, u32[]{:S(2)}) copy-start(f32[6144,512]{0,1:T(8,128)} %fusion.29) | copy-start | bytes 37748740 | tf_op jit(solution)/shard_map/while
  259.9 10.4 %copy-start = (f32[6144,512]{0,1:T(8,128)S(1)}, f32[6144,512]{0,1:T(8,128)}, u32[]{:S(2)}) copy-start(f32[6144,512]{0,1:T(8,128)} %fusion.29) | copy-start | bytes 37748740 | tf_op jit(solution)/shard_map/while
  307.1 10.4 %copy-start = (f32[6144,512]{0,1:T(8,128)S(1)}, f32[6144,512]{0,1:T(8,128)}, u32[]{:S(2)}) copy-start(f32[6144,512]{0,1:T(8,128)} %fusion.29) | copy-start | bytes 37748740 | tf_op jit(solution)/shard_map/while
  354.4 10.4 %copy-start = (f32[6144,512]{0,1:T(8,128)S(1)}, f32[6144,512]{0,1:T(8,128)}, u32[]{:S(2)}) copy-start(f32[6144,512]{0,1:T(8,128)} %fusion.29) | copy-start | bytes 37748740 | tf_op jit(solution)/shard_map/while
  401.7 10.4 %copy-start = (f32[6144,512]{0,1:T(8,128)S(1)}, f32[6144,512]{0,1:T(8,128)}, u32[]{:S(2)}) copy-start(f32[6144,512]{0,1:T(8,128)} %fusion.29) | copy-start | bytes 37748740 | tf_op jit(solution)/shard_map/while
  431.6 0.8 copy-start.1
  432.4 204.3 %reduce-scatter.5.cloned.1.call-start = ((), (), s32[]{:S(2)}) async-start(), calls=%async_computation.3 | async-start | bytes 835584 | tf_op jit(solution)/shard_map/reduce_scatter | solution.py:99
  573.6 64.6 %copy-start.4 = (f32[17,384]{1,0:T(8,128)}, f32[17,384]{1,0:T(8,128)S(1)}, u32[]{:S(2)}) copy-start(f32[17,384]{1,0:T(8,128)S(1)} %get-tuple-element.151) | copy-start | bytes 78340
Sparse Core Ops, SparseCore 0:
  432.5 69.7 reduce-scatter.2
  504.7 60.5 reduce-scatter.4
where the time goes:
time: 646 us; the launch traced here: 645 us
  blocking collectives  266 us (41%)
  matrix products  266 us (41%)
  waiting for transfers between devices  66.9 us (10%)
  local copies, waits for them, and re-layouts  17.4 us (3%)
  between operations  14.8 us (2%)
  other arithmetic  13.2 us (2%)
    dot_general x6, matrix products, tile_update(): jnp.einsum('dr,dc->rc', row_scaled, col_scaled, precision=lax.Precision.H...  98.3 us
    psum x1, blocking collectives, on_device(): norm_now = lax.psum(jnp.sum(residual * residual, axis=1), ('row', 'col'))  68.7 us
    reduce_scatter x1, waiting for transfers between devices, on_device(): lax.psum_scatter(row_partial[0], 'col', scatter_dimension=1, tiled=True)  66.9 us
    dot_general x6, matrix products, tile_update(): jnp.einsum('sr,sc->rc', row_iterate, col_coeff, precision=lax.Precision.H...  66.4 us
    psum x1, blocking collectives, on_device(): lax.psum(jnp.sum(residual_next * residual_next, axis=1), ('row', 'col'))  62.4 us
    dot_general x6, matrix products, tile_update(): jnp.einsum('sc,rc->sr', col_direction, kernel, precision=lax.Precision.HI...  55.3 us
    dot_general x6, matrix products, tile_update(): jnp.einsum('dc,rc->dr', stacked, energy, precision=lax.Precision.HIGHEST)  45.8 us
    all_gather x1, blocking collectives, on_device(): lax.all_gather(scaled, 'row', axis=1, tiled=True)  29.2 us
  transfers between devices with their start and end apart: 2, of which 1 were waited for; matrix products, arithmetic and copies ran while one was open for 1% of the time, Pallas kernels for 0%

commit v1 on v0

v1 whole, which is shorter than its diff:
```python
import functools
import math

import jax
import jax.numpy as jnp
from jax import lax
from jax.experimental import pallas as pl
from jax.experimental.pallas import tpu as pltpu
from jax.sharding import PartitionSpec as P

F32 = jnp.float32
BF16 = jnp.bfloat16
MESH = pl.DeviceIdType.MESH
LOG2E = math.log2(math.e)

ROWS = 8
CHIPS = 8
B = 384
UNIT_R = 2
CP = 72
RP = 56
DR = 24
MB = 48
MX = 176
MXL = 144
PART = 56


def dot(a, b):
    return lax.dot_general(a, b, (((1,), (0,)), ((), ())), preferred_element_type=F32)


def high(v):
    return v.astype(BF16).astype(F32)


def split(v):
    h = v.astype(BF16)
    return h, (v - h.astype(F32)).astype(BF16)


def norm_rows(first, second):
    lane = lax.broadcasted_iota(jnp.int32, (8, B), 0)
    s = -0.5 * jnp.sum(first * first + 2.0 * first * second, axis=0, keepdims=True)
    s0 = high(s)
    s1 = high(s - s0)
    s2 = s - s0 - s1
    parts = jnp.where(lane % 3 == 0, s0, jnp.where(lane % 3 == 1, s1, s2))
    return lane, parts


def prep_column(block, at, eye, fct, wct, dmat, xmat):
    y = block[0:32, :]
    yh = high(y)
    yl = high(y - yh)
    lane, parts = norm_rows(yh, yl)
    tail = jnp.where(lane < 3, parts, jnp.where(lane < 6, 1.0, 0.0))
    zeros = jnp.zeros((24, B), F32)
    c = block[32:56, :]
    ch = high(c)
    cl = c - ch
    feats = jnp.concatenate([yh, yl, yh, tail, zeros], axis=0).astype(BF16)
    wfeat = jnp.concatenate([ch, cl, ch, jnp.zeros((56, B), F32)], axis=0).astype(BF16)
    both = jnp.concatenate([feats, wfeat], axis=0)
    for j in range(B // 128):
        turned = lax.dot_general(
            eye, both[:, j * 128 : (j + 1) * 128], (((1,), (1,)), ((), ())), preferred_element_type=F32
        ).astype(BF16)
        rows = pl.ds(pl.multiple_of(at + j * 128, 128), 128)
        fct[rows, :] = turned[:, :128]
        wct[rows, :] = turned[:, 128:]
    cols = pl.ds(pl.multiple_of(at, 128), B)
    d = block[48:72, :]
    dh = high(d)
    dmat[:, cols] = jnp.concatenate([dh, d - dh], axis=0).astype(BF16)
    exact = yh + yl
    q = exact * exact
    q0 = high(q)
    q1 = high(q - q0)
    q2 = q - q0 - q1
    one = jnp.where(lax.broadcasted_iota(jnp.int32, (16, B), 0) == 0, 1.0, 0.0)
    xmat[:, cols] = jnp.concatenate([one, yh, yl, q0, q1, q2], axis=0).astype(BF16)


def prep_row(block, at, frm, wrm):
    y = block[0:32, :]
    yh = high(y)
    yl = high(y - yh)
    lane, parts = norm_rows(yh, yl)
    tail = jnp.where(lane < 3, 1.0, jnp.where(lane < 6, parts, 0.0))
    cols = pl.ds(pl.multiple_of(at, 128), B)
    frm[:, cols] = jnp.concatenate([yh, yh, yl, tail, jnp.zeros((24, B), F32)], axis=0).astype(BF16)
    c = block[32:56, :]
    ch = high(c)
    wrm[:, cols] = jnp.concatenate([ch, ch, c - ch, jnp.zeros((56, B), F32)], axis=0).astype(BF16)


ROW_STEPS = ((0, 0), (1, 0), (3, 0), (2, 0), (0, 1), (1, 1), (3, 1), (2, 1))
CHIP_STEPS = ((0, 0), (1, 0), (3, 0), (0, 1), (2, 0), (1, 1), (3, 1), (2, 1))


def kernel(
    points, lengths, amp, noise, rhs, iterate, residual, direction, ki_out, grad_out, stat_out,
    cpack, rpack, cbuf, rbuf, fct, wct, dmat, xmat, frm, wrm, accb, accx, part, red, statr, statc, tot,
    c_send, c_recv, f_send, f_recv, r_send, r_recv, p_send, p_recv, s_send, s_recv, t_send, t_recv,
):
    row = lax.axis_index("row")
    col = lax.axis_index("col")
    core = col % 2
    x = (col // 2) % 4
    z = col // 8
    mate = (row, z * 8 + x * 2 + (1 - core))

    def chip_to(k):
        dx, dz = CHIP_STEPS[k]
        return (row, ((z + dz) % 2) * 8 + ((x + dx) % 4) * 2 + core)

    def row_to(slot):
        dy, dz = ROW_STEPS[slot]
        return (((row // 2 + dy) % 4) * 2 + (row + dz) % 2, col)

    def row_from(slot):
        turn = slot % 4
        dy = turn + (turn // 2) * (1 - 2 * (turn % 2))
        return (((row // 2 + 4 - dy) % 4) * 2 + (row + slot // 4) % 2, col)

    barrier = pltpu.get_barrier_semaphore()
    for slot in range(1, ROWS):
        pl.semaphore_signal(barrier, inc=1, device_id=row_to(slot), device_id_type=MESH)
    for o in range(1, 2 * CHIPS):
        pl.semaphore_signal(barrier, inc=1, device_id=(row, (col + o) % 16), device_id_type=MESH)

    wide = jnp.broadcast_to(lengths[...], (32, 32))
    diagonal = lax.broadcasted_iota(jnp.int32, (32, 32), 0) == lax.broadcasted_iota(jnp.int32, (32, 32), 1)
    length = jnp.sum(jnp.where(diagonal, wide, 0.0), axis=1, keepdims=True)
    y = points[...] * (math.sqrt(LOG2E) / length)
    rpack[0:32, :] = y
    rpack[32:48, :] = iterate[1:17, :]
    rpack[48:49, :] = iterate[0:1, :]
    rpack[49:RP, :] = jnp.zeros((RP - 49, B), F32)
    cpack[0:32, :] = y
    cpack[32:48, :] = rhs[1:17, :] * (-1.0 / 16.0)
    cpack[48:49, :] = iterate[0:1, :]
    cpack[49:66, :] = direction[...]
    cpack[66:CP, :] = jnp.zeros((CP - 66, B), F32)
    pl.semaphore_wait(barrier, ROWS - 1 + 2 * CHIPS - 1)

    def send(src, dst, ssem, rsem, to):
        return pltpu.make_async_remote_copy(
            src_ref=src, dst_ref=dst, send_sem=ssem, recv_sem=rsem, device_id=to, device_id_type=MESH
        )

    def row_copy(slot, to):
        return send(rpack, rbuf.at[slot - 1], r_send.at[slot - 1], r_recv.at[slot - 1], to)

    def chip_copy(k, to):
        return send(cpack, cbuf.at[2 * k], c_send.at[k], c_recv.at[k], to)

    def forward(k):
        return send(cbuf.at[2 * k], cbuf.at[2 * k + 1], f_send.at[k], f_recv.at[k], mate)

    def relay(k):
        chip_copy(k, mate).wait_recv()
        forward(k).start()

    own_copies = [send(cpack, cbuf.at[1], c_send.at[0], c_recv.at[0], mate)]
    own_copies += [chip_copy(k, chip_to(k)) for k in range(1, CHIPS)]
    row_copies = [row_copy(slot, row_to(slot)) for slot in range(1, ROWS)]
    for copy in row_copies[:1] + own_copies[:1] + row_copies[1:] + own_copies[1:]:
        copy.start()

    eye = jnp.where(
        lax.broadcasted_iota(jnp.int32, (128, 128), 0) == lax.broadcasted_iota(jnp.int32, (128, 128), 1), 1.0, 0.0
    ).astype(BF16)
    accb[...] = jnp.zeros(accb.shape, F32)
    accx[...] = jnp.zeros(accx.shape, F32)

    def column(block, slot):
        prep_column(block, slot * B, eye, fct, wct, dmat, xmat)

    def row_in(slot):
        row_copy(slot, mate).wait_recv()
        prep_row(rbuf.at[slot - 1], slot * B, frm, wrm)

    def chip_in(k):
        column(cbuf.at[2 * k], 2 * k)
        forward(k).wait_recv()
        column(cbuf.at[2 * k + 1], 2 * k + 1)

    TR = UNIT_R * B

    def tile(u, first, width):
        rs = pl.ds(pl.multiple_of(u * TR, TR), TR)
        cs = pl.ds(pl.multiple_of(first, 2 * B), width)
        value = jnp.exp2(dot(fct[cs, :], frm[:, rs]))
        h, l = split(value)
        accb[:, rs] += dot(dmat[:, cs], h)
        accb[0:32, rs] += dot(dmat[0:32, cs], l)
        h, l = split(value * dot(wct[cs, :], wrm[:, rs]))
        accx[:, rs] += dot(xmat[:, cs], h)
        accx[0:MXL, rs] += dot(xmat[0:MXL, cs], l)

    column(cpack, 0)
    prep_row(rpack, 0, frm, wrm)
    own_copies[0].wait_recv()
    column(cbuf.at[1], 1)
    row_in(1)
    UNITS = ROWS // UNIT_R

    def pass_own(u, carry):
        tile(u, 0, 2 * B)

        @pl.when(u < UNITS - 1)
        def _():
            row_in(2 * u + 2)
            row_in(2 * u + 3)

        @pl.when(u == 2)
        def _():
            relay(1)

        return carry

    lax.fori_loop(0, UNITS, pass_own, 0)
    chip_in(1)

    def pass_one(u, carry):
        @pl.when(u == 0)
        def _():
            relay(2)

        @pl.when(u == 2)
        def _():
            relay(3)

        tile(u, 2 * B, 2 * B)
        return carry

    lax.fori_loop(0, UNITS, pass_one, 0)
    chip_in(2)
    chip_in(3)

    def pass_two(u, carry):
        relay(4 + u)
        tile(u, 4 * B, 4 * B)
        return carry

    lax.fori_loop(0, UNITS, pass_two, 0)
    for k in range(4, CHIPS):
        chip_in(k)

    def ship(slot):
        return send(part.at[slot], red.at[slot - 1], p_send.at[slot - 1], p_recv.at[slot - 1], row_from(slot))

    def pass_last(step, carry):
        u = UNITS - 1 - step

        def half(v, inner):
            tile(u, 8 * B + v * (4 * B), 4 * B)
            return inner

        lax.fori_loop(0, 2, half, 0)
        for j in reversed(range(UNIT_R)):
            slot = u * UNIT_R + j
            cols = pl.ds(pl.multiple_of(slot * B, 128), B)
            y = frm[0:32, cols].astype(F32) + frm[64:96, cols].astype(F32)
            part[slot, 0:DR, :] = accb[0:DR, cols] + accb[DR : 2 * DR, cols]
            weight = accx[0:1, cols]
            first = accx[16:48, cols] + accx[48:80, cols]
            second = accx[80:112, cols] + accx[112:144, cols] + accx[144:176, cols]
            part[slot, DR:PART, :] = y * y * weight - 2.0 * y * first + second
            if j:
                ship(slot).start()
            else:

                @pl.when(u > 0)
                def _():
                    ship(slot).start()

        return carry

    lax.fori_loop(0, UNITS, pass_last, 0)

    d = cpack[48:72, :]
    r = jnp.concatenate([jnp.zeros((1, B), F32), residual[...], jnp.zeros((DR - 18, B), F32)], axis=0)
    product = part[0, 0:DR, :]
    grad = part[0, DR:PART, :]
    for slot in reversed(range(1, ROWS)):
        ship(slot).wait_recv()
        product = product + red[slot - 1, 0:DR, :]
        grad = grad + red[slot - 1, DR:PART, :]
    image = amp[0] * product + noise[0] * d
    ki_out[...] = image
    grad_out[...] = grad

    place = lax.broadcasted_iota(jnp.int32, (DR, 128), 1)
    stats = jnp.zeros((DR, 128), F32)
    for at, value in enumerate((r * r, d * image, r * image, image * image)):
        stats = jnp.where(place == at, jnp.sum(value, axis=1, keepdims=True), stats)
    tot[0] = stats

    def tell_row(slot):
        return send(tot.at[0], statr.at[slot - 1], s_send.at[slot - 1], s_recv.at[slot - 1], row_to(slot))

    def tell_col(o):
        return send(tot.at[1], statc.at[o - 1], t_send.at[o - 1], t_recv.at[o - 1], (row, (col + o) % 16))

    for slot in reversed(range(1, ROWS)):
        tell_row(slot).start()
    for slot in range(1, ROWS):
        tell_row(slot).wait_recv()
        stats = stats + statr[slot - 1]
    tot[1] = stats
    for o in range(1, 2 * CHIPS):
        tell_col(o).start()
    for o in range(1, 2 * CHIPS):
        tell_col(o).wait_recv()
        stats = stats + statc[o - 1]
    stat_out[...] = stats

    for copy in own_copies + row_copies:
        copy.wait_send()
    for k in range(1, CHIPS):
        forward(k).wait_send()
    for slot in range(1, ROWS):
        ship(slot).wait_send()
        tell_row(slot).wait_send()
    for o in range(1, 2 * CHIPS):
        tell_col(o).wait_send()


def on_device(points, lengthscale, outputscale, noise, rhs, iterate, residual, direction):
    systems = rhs.shape[0]
    vmem = pl.BlockSpec(memory_space=pltpu.VMEM)
    smem = pl.BlockSpec(memory_space=pltpu.SMEM)
    points_c = 2 * CHIPS * B
    points_r = ROWS * B
    dma = pltpu.SemaphoreType.DMA
    image, grad, stats = pl.pallas_call(
        kernel,
        out_shape=[
            jax.ShapeDtypeStruct((DR, B), F32),
            jax.ShapeDtypeStruct((32, B), F32),
            jax.ShapeDtypeStruct((DR, 128), F32),
        ],
        in_specs=[vmem, vmem, smem, smem, vmem, vmem, vmem, vmem],
        out_specs=[vmem, vmem, vmem],
        scratch_shapes=[
            pltpu.VMEM((CP, B), F32),
            pltpu.VMEM((RP, B), F32),
            pltpu.VMEM((2 * CHIPS, CP, B), F32),
            pltpu.VMEM((ROWS - 1, RP, B), F32),
            pltpu.VMEM((points_c, 128), BF16),
            pltpu.VMEM((points_c, 128), BF16),
            pltpu.VMEM((MB, points_c), BF16),
            pltpu.VMEM((MX, points_c), BF16),
            pltpu.VMEM((128, points_r), BF16),
            pltpu.VMEM((128, points_r), BF16),
            pltpu.VMEM((MB, points_r), F32),
            pltpu.VMEM((MX, points_r), F32),
            pltpu.VMEM((ROWS, PART, B), F32),
            pltpu.VMEM((ROWS - 1, PART, B), F32),
            pltpu.VMEM((ROWS - 1, DR, 128), F32),
            pltpu.VMEM((2 * CHIPS - 1, DR, 128), F32),
            pltpu.VMEM((2, DR, 128), F32),
            dma((CHIPS,)),
            dma((CHIPS,)),
            dma((CHIPS,)),
            dma((CHIPS,)),
            dma((ROWS - 1,)),
            dma((ROWS - 1,)),
            dma((ROWS - 1,)),
            dma((ROWS - 1,)),
            dma((ROWS - 1,)),
            dma((ROWS - 1,)),
            dma((2 * CHIPS - 1,)),
            dma((2 * CHIPS - 1,)),
        ],
        compiler_params=pltpu.CompilerParams(
            collective_id=0, has_side_effects=True, vmem_limit_bytes=56 << 20
        ),
        name="cg_step",
    )(points, lengthscale[None, :], outputscale, noise, rhs, iterate, residual, direction)

    live = slice(1, 1 + systems)
    image = image[live]
    norm_now, curvature, cross, square = (stats[live, j : j + 1] for j in range(4))
    step = norm_now / curvature
    norm_next = jnp.maximum(norm_now - 2.0 * step * cross + step * step * square, 0.0)
    residual_next = residual - step * image
    iterate_next = iterate + step * direction
    direction_next = residual_next + (norm_next / (norm_now + 1e-06)) * direction
    length_terms = ((0.5 / LOG2E) * outputscale[0] / lengthscale)[:, None] * grad
    return (iterate_next, residual_next, direction_next, length_terms)


def solution(mesh):
    spread = P(None, ("row", "col"))
    return jax.shard_map(
        on_device,
        mesh=mesh,
        in_specs=(spread, P(), P(), P(), spread, spread, spread, spread),
        out_specs=(spread, spread, spread, spread),
        check_vma=False,
    )
```

time: 646 us -> 97.4 us (0.15)
  matrix products: 266 us -> 0 us
  blocking collectives: 266 us -> 0 us
  Pallas kernels: 0 us -> 91.2 us
  waiting for transfers between devices: 66.9 us -> 0 us
  local copies, waits for them, and re-layouts: 17.4 us -> 0.67 us
  between operations: 14.8 us -> 1.99 us
  other arithmetic: 13.2 us -> 3.28 us
    dot_general x24 -> x0, matrix products: 266 us -> none  [the longest x6 98.3 us: tile_update(): jnp.einsum('dr,dc->rc', row_scaled, col_scaled, precision=lax.Precision.H...]
    all_gather x5 -> x0, blocking collectives: 135 us -> none  [the longest x1 29.2 us: on_device(): lax.all_gather(scaled, 'row', axis=1, tiled=True)]
    psum x2 -> x0, blocking collectives: 131 us -> none  [the longest x1 68.7 us: on_device(): norm_now = lax.psum(jnp.sum(residual * residual, axis=1), ('row', 'col'))]
    pallas_call x0 -> x1, Pallas kernels: none -> 91.2 us  [on_device(): pl.pallas_call(kernel, out_shape=[jax.ShapeDtypeStruct((DR, B), F32), jax...]
    reduce_scatter x2 -> x0, waiting for transfers between devices: 66.9 us -> none  [the longest x1 66.9 us: on_device(): lax.psum_scatter(row_partial[0], 'col', scatter_dimension=1, tiled=True)]
    dynamic_slice x18 -> x0, local copies, waits for them, and re-layouts: 13.9 us -> none  [fold_columns(): lax.scan(scan_step, totals, (split_cols(col_scaled), split_cols(col_direc...]
  transfers between devices with their start and end apart: 2 -> 0, of which waited for: 1 -> 0; matrix products, arithmetic and copies ran while one was open for 1% -> 0% of each run, Pallas kernels for 0% -> 0%
where the time goes in v1:
time: 97.4 us; the launch traced here: 97.1 us
  Pallas kernels  91.2 us (94%)
  other arithmetic  3.28 us (3%)
  between operations  1.99 us (2%)
    pallas_call x1, Pallas kernels, on_device(): pl.pallas_call(kernel, out_shape=[jax.ShapeDtypeStruct((DR, B), F32), jax...  91.2 us

profile of v1, /device:TPU:1, one launch (start us, length us, event | category | flops | bytes accessed | tf_op | source)
XLA Modules:
  0.0 97.1 jit_solution(10656166929538759001)
XLA Ops:
  1.9 0.0 copy-start.4
  1.9 0.6 copy-done.4
  2.6 91.2 %cg_step.1 = (f32[24,384]{1,0:T(8,128)}, f32[32,384]{1,0:T(8,128)}, f32[24,128]{1,0:T(8,128)}) custom-call(f32[32,384]{1,0:T(8,128)} %points.1, f32[1,32]{1,0:T(1,128)} %bitcast.2, f32[1]{0:T(128)S(6)} %copy.12.amp, f32[1]{0:T(128)S(6)} %copy.13.noise, f32[17,384]{1,0:T(8,128)} %rhs.3, f32[17,384]{1,0:T(8,128)} %iterate.1, f32[17,384]{1,0:T(8,128)} %residual.1, ...), custom_call_target="tpu_custom_call" | custom-call | tf_op jit(solution)/shard_map/cg_step/pallas_call | solution.py:339
  93.8 0.0 copy-start.2
  93.8 0.0 copy-start.3
  93.8 1.0 %fusion = (f32[17]{0:T(128)S(1)}, f32[17]{0:T(128)S(1)}) fusion(f32[24,128]{1,0:T(8,128)} %get-tuple-element.7), kind=kLoop, calls=%fused_computation.6 | loop fusion | flops 170 | bytes 408 | tf_op jit(solution)/shard_map/div | solution.py:392
  94.8 0.0 copy-start
  94.8 0.0 copy-start.1
  94.9 1.5 %broadcast_multiply_fusion = f32[32,384]{1,0:T(8,128)} fusion(f32[32,384]{1,0:T(8,128)} %get-tuple-element.9, f32[32]{0:T(128)S(1)} %broadcast_divide_fusion), kind=kLoop, calls=%fused_computation.3 | loop fusion | flops 12288 | bytes 98432 | tf_op jit(solution)/shard_map/mul | solution.py:393
  96.4 0.0 copy-done.2
  96.4 0.0 copy-done.3
  96.4 0.0 copy-done
  96.4 0.0 copy-done.1
  96.4 0.7 multiply_add_fusion
  (1 shorter events, 0.0 us)
Async XLA Ops:
  1.9 0.7 copy-start.4
  93.8 2.6 %copy-start.2 = (f32[17,384]{1,0:T(8,128)S(1)}, f32[17,384]{1,0:T(8,128)}, u32[]{:S(2)}) copy-start(f32[17,384]{1,0:T(8,128)} %residual.1) | copy-start | bytes 78340
  93.8 2.6 %copy-start.3 = (f32[24,384]{1,0:T(8,128)S(1)}, f32[24,384]{1,0:T(8,128)}, u32[]{:S(2)}) copy-start(f32[24,384]{1,0:T(8,128)} %get-tuple-element.8) | copy-start | bytes 110596
  94.8 1.5 %copy-start = (f32[17,384]{1,0:T(8,128)S(1)}, f32[17,384]{1,0:T(8,128)}, u32[]{:S(2)}) copy-start(f32[17,384]{1,0:T(8,128)} %direction.1) | copy-start | bytes 78340
  94.8 1.5 %copy-start.1 = (f32[17,384]{1,0:T(8,128)S(1)}, f32[17,384]{1,0:T(8,128)}, u32[]{:S(2)}) copy-start(f32[17,384]{1,0:T(8,128)} %iterate.1) | copy-start | bytes 78340

commit v2 on v1

--- a/solution.py
+++ b/solution.py
@@ -100,7 +100,7 @@
 
 
 def kernel(
-    points, lengths, amp, noise, rhs, iterate, residual, direction, ki_out, grad_out, stat_out,
+    points, lengths, amp, noise, rhs, iterate, residual, direction, iterate_out, residual_out, direction_out, terms_out,
     cpack, rpack, cbuf, rbuf, fct, wct, dmat, xmat, frm, wrm, accb, accx, part, red, statr, statc, tot,
     c_send, c_recv, f_send, f_recv, r_send, r_recv, p_send, p_recv, s_send, s_recv, t_send, t_recv,
 ):
@@ -290,13 +290,14 @@
         product = product + red[slot - 1, 0:DR, :]
         grad = grad + red[slot - 1, DR:PART, :]
     image = amp[0] * product + noise[0] * d
-    ki_out[...] = image
-    grad_out[...] = grad
-
-    place = lax.broadcasted_iota(jnp.int32, (DR, 128), 1)
-    stats = jnp.zeros((DR, 128), F32)
+    terms_out[...] = ((0.5 / LOG2E) * amp[0] / length) * grad
+
+    place = lax.broadcasted_iota(jnp.int32, (8, 128), 0)
+    corner = lax.broadcasted_iota(jnp.int32, (DR, 128), 0) == lax.broadcasted_iota(jnp.int32, (DR, 128), 1)
+    stats = jnp.zeros((8, 128), F32)
     for at, value in enumerate((r * r, d * image, r * image, image * image)):
-        stats = jnp.where(place == at, jnp.sum(value, axis=1, keepdims=True), stats)
+        total = jnp.where(corner, jnp.sum(value, axis=1, keepdims=True), 0.0)
+        stats = jnp.where(place == at, jnp.sum(total, axis=0, keepdims=True), stats)
     tot[0] = stats
 
     def tell_row(slot):
@@ -316,7 +317,20 @@
     for o in range(1, 2 * CHIPS):
         tell_col(o).wait_recv()
         stats = stats + statc[o - 1]
-    stat_out[...] = stats
+
+    norm_now, curvature, cross, square = (stats[j : j + 1, :] for j in range(4))
+    step = norm_now / curvature
+    norm_next = jnp.maximum(norm_now - 2.0 * step * cross + step * step * square, 0.0)
+    ratio = norm_next / (norm_now + 1e-06)
+
+    def upright(line):
+        return jnp.sum(jnp.where(corner, line, 0.0), axis=1, keepdims=True)[1:18, :]
+
+    step = upright(step)
+    residual_next = residual[...] - step * image[1:18, :]
+    iterate_out[...] = iterate[...] + step * direction[...]
+    residual_out[...] = residual_next
+    direction_out[...] = residual_next + upright(ratio) * direction[...]
 
     for copy in own_copies + row_copies:
         copy.wait_send()
@@ -330,21 +344,21 @@
 
 
 def on_device(points, lengthscale, outputscale, noise, rhs, iterate, residual, direction):
-    systems = rhs.shape[0]
     vmem = pl.BlockSpec(memory_space=pltpu.VMEM)
     smem = pl.BlockSpec(memory_space=pltpu.SMEM)
     points_c = 2 * CHIPS * B
     points_r = ROWS * B
     dma = pltpu.SemaphoreType.DMA
-    image, grad, stats = pl.pallas_call(
+    return tuple(pl.pallas_call(
         kernel,
         out_shape=[
-            jax.ShapeDtypeStruct((DR, B), F32),
+            jax.ShapeDtypeStruct((17, B), F32),
+            jax.ShapeDtypeStruct((17, B), F32),
+            jax.ShapeDtypeStruct((17, B), F32),
             jax.ShapeDtypeStruct((32, B), F32),
-            jax.ShapeDtypeStruct((DR, 128), F32),
         ],
         in_specs=[vmem, vmem, smem, smem, vmem, vmem, vmem, vmem],
-        out_specs=[vmem, vmem, vmem],
+        out_specs=[vmem, vmem, vmem, vmem],
         scratch_shapes=[
             pltpu.VMEM((CP, B), F32),
             pltpu.VMEM((RP, B), F32),
@@ -360,9 +374,9 @@
             pltpu.VMEM((MX, points_r), F32),
             pltpu.VMEM((ROWS, PART, B), F32),
             pltpu.VMEM((ROWS - 1, PART, B), F32),
-            pltpu.VMEM((ROWS - 1, DR, 128), F32),
-            pltpu.VMEM((2 * CHIPS - 1, DR, 128), F32),
-            pltpu.VMEM((2, DR, 128), F32),
+            pltpu.VMEM((ROWS - 1, 8, 128), F32),
+            pltpu.VMEM((2 * CHIPS - 1, 8, 128), F32),
+            pltpu.VMEM((2, 8, 128), F32),
             dma((CHIPS,)),
             dma((CHIPS,)),
             dma((CHIPS,)),
@@ -380,18 +394,7 @@
             collective_id=0, has_side_effects=True, vmem_limit_bytes=56 << 20
         ),
         name="cg_step",
-    )(points, lengthscale[None, :], outputscale, noise, rhs, iterate, residual, direction)
-
-    live = slice(1, 1 + systems)
-    image = image[live]
-    norm_now, curvature, cross, square = (stats[live, j : j + 1] for j in range(4))
-    step = norm_now / curvature
-    norm_next = jnp.maximum(norm_now - 2.0 * step * cross + step * step * square, 0.0)
-    residual_next = residual - step * image
-    iterate_next = iterate + step * direction
-    direction_next = residual_next + (norm_next / (norm_now + 1e-06)) * direction
-    length_terms = ((0.5 / LOG2E) * outputscale[0] / lengthscale)[:, None] * grad
-    return (iterate_next, residual_next, direction_next, length_terms)
+    )(points, lengthscale[None, :], outputscale, noise, rhs, iterate, residual, direction))
 
 
 def solution(mesh):

time: 97.4 us -> 96.8 us (level)
  other arithmetic: 3.28 us -> 0 us
  local copies, waits for them, and re-layouts: 0.67 us -> 3.61 us
    unnamed x10, local copies, waits for them, and re-layouts: 0.67 us -> 3.61 us
    mul x1 -> x0, other arithmetic: 1.51 us -> none  [on_device(): length_terms = (0.5 / LOG2E * outputscale[0] / lengthscale)[:, None] * grad]
    div x2 -> x0, other arithmetic: 1.05 us -> none  [the longest x1 1.05 us: on_device(): direction_next = residual_next + norm_next / (norm_now + 1e-06) * direction]
where the time goes in v2:
time: 96.8 us; the launch traced here: 96.4 us
  Pallas kernels  90.9 us (94%)
  local copies, waits for them, and re-layouts  3.61 us (4%)
  between operations  1.94 us (2%)
    pallas_call x1, Pallas kernels, on_device(): pl.pallas_call(kernel, out_shape=[jax.ShapeDtypeStruct((17, B), F32), jax...  90.9 us
    unnamed x10, local copies, waits for them, and re-layouts  3.61 us

profile of v2, /device:TPU:1, one launch (start us, length us, event | category | flops | bytes accessed | tf_op | source)
XLA Modules:
  0.0 96.4 jit_solution(6671992683085209031)
XLA Ops:
  1.9 90.9 %cg_step.1 = (f32[17,384]{1,0:T(8,128)}, f32[17,384]{1,0:T(8,128)}, f32[17,384]{1,0:T(8,128)}, f32[32,384]{1,0:T(8,128)}) custom-call(f32[32,384]{1,0:T(8,128)} %points.1, f32[1,32]{1,0:T(1,128)} %bitcast.1, f32[1]{0:T(128)S(6)} %copy.16.amp, f32[1]{0:T(128)S(6)} %copy.17.noise, f32[17,384]{1,0:T(8,128)} %rhs.1, f32[17,384]{1,0:T(8,128)} %iterate.1, ...), custom_call_target="tpu_custom_call" | custom-call | tf_op jit(solution)/shard_map/cg_step/pallas_call | solution.py:352
  92.8 0.0 copy-start.2
  92.8 1.4 %copy.18 = f32[17,384]{1,0:T(8,128)} copy(f32[17,384]{1,0:T(8,128)} %get-tuple-element.8) | data formatting | bytes 52224
  94.2 0.0 copy-done.2
  94.2 0.0 copy-start.1
  94.2 0.6 copy.19
  94.8 0.2 copy-done.1
  95.0 0.0 copy-start
  95.0 0.6 copy.20
  95.6 0.2 copy-done
  95.8 0.6 copy.21
Async XLA Ops:
  92.8 1.4 %copy-start.2 = (f32[17,384]{1,0:T(8,128)S(1)}, f32[17,384]{1,0:T(8,128)}, u32[]{:S(2)}) copy-start(f32[17,384]{1,0:T(8,128)} %get-tuple-element.9) | copy-start | bytes 78340
  94.2 0.8 copy-start.1
  95.0 0.8 copy-start

commit v3 on v2

--- a/solution.py
+++ b/solution.py
@@ -23,7 +23,7 @@
 MB = 48
 MX = 176
 MXL = 144
-PART = 56
+LATE = 2
 
 
 def dot(a, b):
@@ -101,8 +101,8 @@
 
 def kernel(
     points, lengths, amp, noise, rhs, iterate, residual, direction, iterate_out, residual_out, direction_out, terms_out,
-    cpack, rpack, cbuf, rbuf, fct, wct, dmat, xmat, frm, wrm, accb, accx, part, red, statr, statc, tot,
-    c_send, c_recv, f_send, f_recv, r_send, r_recv, p_send, p_recv, s_send, s_recv, t_send, t_recv,
+    cpack, rpack, cbuf, rbuf, fct, wct, dmat, xmat, frm, wrm, accb, accx, keep, partp, partg, redp, redg, statr, statc, tot, image_ref,
+    c_send, c_recv, f_send, f_recv, r_send, r_recv, p_send, p_recv, g_send, g_recv, s_send, s_recv, t_send, t_recv,
 ):
     row = lax.axis_index("row")
     col = lax.axis_index("col")
@@ -249,48 +249,91 @@
     for k in range(4, CHIPS):
         chip_in(k)
 
-    def ship(slot):
-        return send(part.at[slot], red.at[slot - 1], p_send.at[slot - 1], p_recv.at[slot - 1], row_from(slot))
-
-    def pass_last(step, carry):
-        u = UNITS - 1 - step
-
+    def tile_product(u, v, rs, cs):
+        value = jnp.exp2(dot(fct[cs, :], frm[:, rs]))
+        keep[2 * u + v] = value
+        h, l = split(value)
+        accb[:, rs] += dot(dmat[:, cs], h)
+        accb[0:32, rs] += dot(dmat[0:32, cs], l)
+
+    def tile_gradient(u, v, rs, cs):
+        h, l = split(keep[2 * u + v] * dot(wct[cs, :], wrm[:, rs]))
+        accx[:, rs] += dot(xmat[:, cs], h)
+        accx[0:MXL, rs] += dot(xmat[0:MXL, cs], l)
+
+    def halves(u, work):
         def half(v, inner):
-            tile(u, 8 * B + v * (4 * B), 4 * B)
+            rs = pl.ds(pl.multiple_of(u * TR, TR), TR)
+            cs = pl.ds(pl.multiple_of(8 * B + v * (4 * B), 4 * B), 4 * B)
+            work(u, v, rs, cs)
             return inner
 
         lax.fori_loop(0, 2, half, 0)
+
+    def ship_product(slot):
+        return send(partp.at[slot], redp.at[slot - 1], p_send.at[slot - 1], p_recv.at[slot - 1], row_from(slot))
+
+    def ship_gradient(slot):
+        return send(partg.at[slot], redg.at[slot - 1], g_send.at[slot - 1], g_recv.at[slot - 1], row_from(slot))
+
+    def ship(copy, slot, j, u):
+        if j:
+            copy(slot).start()
+        else:
+
+            @pl.when(u > 0)
+            def _():
+                copy(slot).start()
+
+    def products_out(u):
+        for j in reversed(range(UNIT_R)):
+            slot = u * UNIT_R + j
+            cols = pl.ds(pl.multiple_of(slot * B, 128), B)
+            partp[slot] = accb[0:DR, cols] + accb[DR : 2 * DR, cols]
+            ship(ship_product, slot, j, u)
+
+    def gradients_out(u):
         for j in reversed(range(UNIT_R)):
             slot = u * UNIT_R + j
             cols = pl.ds(pl.multiple_of(slot * B, 128), B)
             y = frm[0:32, cols].astype(F32) + frm[64:96, cols].astype(F32)
-            part[slot, 0:DR, :] = accb[0:DR, cols] + accb[DR : 2 * DR, cols]
             weight = accx[0:1, cols]
             first = accx[16:48, cols] + accx[48:80, cols]
             second = accx[80:112, cols] + accx[112:144, cols] + accx[144:176, cols]
-            part[slot, DR:PART, :] = y * y * weight - 2.0 * y * first + second
-            if j:
-                ship(slot).start()
-            else:
-
-                @pl.when(u > 0)
-                def _():
-                    ship(slot).start()
-
-        return carry
-
-    lax.fori_loop(0, UNITS, pass_last, 0)
+            partg[slot] = y * y * weight - 2.0 * y * first + second
+            ship(ship_gradient, slot, j, u)
+
+    def pass_last(step, carry):
+        u = UNITS - 1 - step
+        halves(u, lambda u, v, rs, cs: tile(u, 8 * B + v * (4 * B), 4 * B))
+        products_out(u)
+        gradients_out(u)
+        return carry
+
+    def pass_product(step, carry):
+        u = LATE - 1 - step
+        halves(u, tile_product)
+        products_out(u)
+        return carry
+
+    def pass_gradient(step, carry):
+        u = LATE - 1 - step
+        halves(u, tile_gradient)
+        gradients_out(u)
+        return carry
+
+    lax.fori_loop(0, UNITS - LATE, pass_last, 0)
+    lax.fori_loop(0, LATE, pass_product, 0)
+    lax.fori_loop(0, LATE - 1, pass_gradient, 0)
 
     d = cpack[48:72, :]
     r = jnp.concatenate([jnp.zeros((1, B), F32), residual[...], jnp.zeros((DR - 18, B), F32)], axis=0)
-    product = part[0, 0:DR, :]
-    grad = part[0, DR:PART, :]
+    product = partp[0]
     for slot in reversed(range(1, ROWS)):
-        ship(slot).wait_recv()
-        product = product + red[slot - 1, 0:DR, :]
-        grad = grad + red[slot - 1, DR:PART, :]
+        ship_product(slot).wait_recv()
+        product = product + redp[slot - 1]
     image = amp[0] * product + noise[0] * d
-    terms_out[...] = ((0.5 / LOG2E) * amp[0] / length) * grad
+    image_ref[...] = image
 
     place = lax.broadcasted_iota(jnp.int32, (8, 128), 0)
     corner = lax.broadcasted_iota(jnp.int32, (DR, 128), 0) == lax.broadcasted_iota(jnp.int32, (DR, 128), 1)
@@ -308,12 +351,21 @@
 
     for slot in reversed(range(1, ROWS)):
         tell_row(slot).start()
+    lax.fori_loop(LATE - 1, LATE, pass_gradient, 0)
+    stats = tot[0]
     for slot in range(1, ROWS):
         tell_row(slot).wait_recv()
         stats = stats + statr[slot - 1]
     tot[1] = stats
     for o in range(1, 2 * CHIPS):
         tell_col(o).start()
+
+    grad = partg[0]
+    for slot in reversed(range(1, ROWS)):
+        ship_gradient(slot).wait_recv()
+        grad = grad + redg[slot - 1]
+    terms_out[...] = ((0.5 / LOG2E) * amp[0] / length) * grad
+    stats = tot[1]
     for o in range(1, 2 * CHIPS):
         tell_col(o).wait_recv()
         stats = stats + statc[o - 1]
@@ -327,7 +379,7 @@
         return jnp.sum(jnp.where(corner, line, 0.0), axis=1, keepdims=True)[1:18, :]
 
     step = upright(step)
-    residual_next = residual[...] - step * image[1:18, :]
+    residual_next = residual[...] - step * image_ref[1:18, :]
     iterate_out[...] = iterate[...] + step * direction[...]
     residual_out[...] = residual_next
     direction_out[...] = residual_next + upright(ratio) * direction[...]
@@ -337,7 +389,8 @@
     for k in range(1, CHIPS):
         forward(k).wait_send()
     for slot in range(1, ROWS):
-        ship(slot).wait_send()
+        ship_product(slot).wait_send()
+        ship_gradient(slot).wait_send()
         tell_row(slot).wait_send()
     for o in range(1, 2 * CHIPS):
         tell_col(o).wait_send()
@@ -372,11 +425,15 @@
             pltpu.VMEM((128, points_r), BF16),
             pltpu.VMEM((MB, points_r), F32),
             pltpu.VMEM((MX, points_r), F32),
-            pltpu.VMEM((ROWS, PART, B), F32),
-            pltpu.VMEM((ROWS - 1, PART, B), F32),
+            pltpu.VMEM((2 * LATE, 4 * B, UNIT_R * B), F32),
+            pltpu.VMEM((ROWS, DR, B), F32),
+            pltpu.VMEM((ROWS, 32, B), F32),
+            pltpu.VMEM((ROWS - 1, DR, B), F32),
+            pltpu.VMEM((ROWS - 1, 32, B), F32),
             pltpu.VMEM((ROWS - 1, 8, 128), F32),
             pltpu.VMEM((2 * CHIPS - 1, 8, 128), F32),
             pltpu.VMEM((2, 8, 128), F32),
+            pltpu.VMEM((DR, B), F32),
             dma((CHIPS,)),
             dma((CHIPS,)),
             dma((CHIPS,)),
@@ -387,11 +444,13 @@
             dma((ROWS - 1,)),
             dma((ROWS - 1,)),
             dma((ROWS - 1,)),
+            dma((ROWS - 1,)),
+            dma((ROWS - 1,)),
             dma((2 * CHIPS - 1,)),
             dma((2 * CHIPS - 1,)),
         ],
         compiler_params=pltpu.CompilerParams(
-            collective_id=0, has_side_effects=True, vmem_limit_bytes=56 << 20
+            collective_id=0, has_side_effects=True, vmem_limit_bytes=60 << 20
         ),
         name="cg_step",
     )(points, lengthscale[None, :], outputscale, noise, rhs, iterate, residual, direction))

time: 96.8 us -> 91.2 us (0.942)
  Pallas kernels: 90.9 us -> 85.3 us
    pallas_call x1, Pallas kernels: 90.9 us -> 85.3 us  [on_device(): pl.pallas_call(kernel, out_shape=[jax.ShapeDtypeStruct((17, B), F32), jax...]
where the time goes in v3:
time: 91.2 us; the launch traced here: 90.9 us
  Pallas kernels  85.3 us (94%)
  local copies, waits for them, and re-layouts  3.61 us (4%)
  between operations  1.94 us (2%)
    pallas_call x1, Pallas kernels, on_device(): pl.pallas_call(kernel, out_shape=[jax.ShapeDtypeStruct((17, B), F32), jax...  85.3 us
    unnamed x10, local copies, waits for them, and re-layouts  3.61 us

profile of v3, /device:TPU:1, one launch (start us, length us, event | category | flops | bytes accessed | tf_op | source)
XLA Modules:
  0.0 90.9 jit_solution(12043380301416484831)
XLA Ops:
  1.9 85.3 %cg_step.1 = (f32[17,384]{1,0:T(8,128)}, f32[17,384]{1,0:T(8,128)}, f32[17,384]{1,0:T(8,128)}, f32[32,384]{1,0:T(8,128)}) custom-call(f32[32,384]{1,0:T(8,128)} %points.1, f32[1,32]{1,0:T(1,128)} %bitcast.1, f32[1]{0:T(128)S(6)} %copy.16.amp, f32[1]{0:T(128)S(6)} %copy.17.noise, f32[17,384]{1,0:T(8,128)} %rhs.1, f32[17,384]{1,0:T(8,128)} %iterate.1, ...), custom_call_target="tpu_custom_call" | custom-call | tf_op jit(solution)/shard_map/cg_step/pallas_call | solution.py:405
  87.3 0.0 copy-start.2
  87.3 1.4 %copy.18 = f32[17,384]{1,0:T(8,128)} copy(f32[17,384]{1,0:T(8,128)} %get-tuple-element.8) | data formatting | bytes 52224
  88.7 0.0 copy-done.2
  88.7 0.0 copy-start.1
  88.7 0.6 copy.19
  89.3 0.2 copy-done.1
  89.4 0.0 copy-start
  89.4 0.6 copy.20
  90.1 0.2 copy-done
  90.3 0.6 copy.21
Async XLA Ops:
  87.3 1.4 %copy-start.2 = (f32[17,384]{1,0:T(8,128)S(1)}, f32[17,384]{1,0:T(8,128)}, u32[]{:S(2)}) copy-start(f32[17,384]{1,0:T(8,128)} %get-tuple-element.9) | copy-start | bytes 78340
  88.7 0.8 copy-start.1
  89.4 0.8 copy-start
